TPU v7x, 32 devices: a whole 2x2x4 slice. The times are simulated.
32 devices in a mesh: dp: 8 (over z, core), ctx: 4 (over y, x).
Axes of the slice: x: 2, y: 2, z: 4, core: 2. Of those that a mesh axis runs over, the one named last changes fastest.
Arguments:
- loader_rows: bfloat16 [8192, 512], P(('dp', 'ctx')), may hold values from -60 to 60
- send_slot: int32 [8192], P(('dp', 'ctx')), may hold values from 0 to 383, as said below
- arrive_slot: int32 [8192], P(('dp', 'ctx')), may hold values from 0 to 383, as said below
- user_lengths: int32 [8, 4], P('dp'), may hold values from 1 to 768, 1024 in all within a row
- proj_weight: bfloat16 [512, 2048], replicated, may hold values from -0.25 to 0.25
- out_weight: bfloat16 [512, 512], replicated, may hold values from -0.25 to 0.25
- cotangent: bfloat16 [8192, 512], P(('dp', 'ctx')), may hold values from -6 to 6
Outputs:
- layer_out: bfloat16 [8192, 512], P(('dp', 'ctx'))
- row_grads: bfloat16 [8192, 512], P(('dp', 'ctx'))
- proj_grad: float32 [512, 2048], replicated
- out_grad: float32 [512, 512], replicated
Inputs may be any that keep to these rules, and one draw needn't show every extreme that they name: `send_slot`: on each loader device its 256 entries are distinct slots d * 12 + k, d the owner device and k counting that owner's rows from this loader from 0; no loader sends more than 12 rows to one owner and some pairs send exactly 12; the number of rows from loader s to owner d depends only on (d - s) mod (8 * 4). `arrive_slot`: on each owner device its 256 entries are distinct slots s * 12 + k, the k-th row that loader s sends to it; every owner receives exactly 256 rows.
All inputs are finite; a program needn't handle non-finite values.
Results may differ from a plain program's by a relative error of at most 0.009.
Values may be sent and summed in bfloat16 or wider, within the bound.
No kernel may reach another device: no remote copies, remote signals or barrier semaphores. Data moves between devices by JAX's collectives and lax.ppermute only.
A program may use at most 128 MiB of HBM per device.

v0:
```python
import jax
import jax.numpy as jnp
from jax import lax
from jax.sharding import PartitionSpec as P

HEADS = 8
norm_eps = 1e-05


def normalize(values):
    centre = values - jnp.mean(values, axis=-1, keepdims=True)
    inverse = lax.rsqrt(jnp.mean(centre * centre, axis=-1, keepdims=True) + norm_eps)
    return (centre * inverse, inverse)


def normalize_back(grad_in, normed, inverse):
    mean_grad = jnp.mean(grad_in, axis=-1, keepdims=True)
    mean_cross = jnp.mean(grad_in * normed, axis=-1, keepdims=True)
    return (grad_in - mean_grad - normed * mean_cross) * inverse


def silu_grad(values):
    sigma = jax.nn.sigmoid(values)
    return sigma * (1.0 + values * (1.0 - sigma))


def in_blocks(step_fn, block_rows, running, pieces):
    total_rows = pieces[0].shape[0]

    def one_block(index, carry):
        start = index * block_rows
        sliced = tuple((lax.dynamic_slice_in_dim(each, start, block_rows, 0) for each in pieces))
        return step_fn(carry, sliced, start)

    return lax.fori_loop(0, total_rows // block_rows, one_block, running)


def local(loader_rows, send_slot, arrive_slot, user_lengths, proj_weight, out_weight, cotangent):
    row_count = send_slot.shape[0]
    model_width = out_weight.shape[0]
    head_dim = model_width // HEADS
    score_scale = head_dim ** (-0.5)
    group_size = lax.axis_size("ctx")
    group_count = lax.axis_size("dp")
    device_count = group_size * group_count
    per_pair = row_count // device_count
    capacity = per_pair + max(1, per_pair // 2)
    half_rows = row_count // 2
    group_total = group_size * row_count
    outgoing = (
        jnp.zeros((device_count * capacity, model_width), jnp.bfloat16)
        .at[send_slot]
        .set(loader_rows)
    )
    arrived = lax.all_to_all(
        outgoing.reshape(device_count, capacity, model_width),
        ("dp", "ctx"),
        split_axis=0,
        concat_axis=0,
        tiled=True,
    )
    own_rows = arrived.reshape(device_count * capacity, model_width)[arrive_slot]
    ends = jnp.cumsum(user_lengths[0])

    def position_of(row_index):
        device_of = row_index // row_count
        local_of = row_index % row_count
        return jnp.where(
            local_of < half_rows,
            device_of * half_rows + local_of,
            group_total - (device_of + 1) * half_rows + (local_of - half_rows),
        )

    own_pos = position_of(
        lax.axis_index("ctx") * row_count + jnp.arange(row_count, dtype=jnp.int32)
    )

    def user_of(positions):
        return jnp.sum((ends[None, :] <= positions[:, None]).astype(jnp.int32), axis=1)

    own_users = user_of(own_pos)

    def allowed_of(query_pos, query_users, key_pos, key_users):
        return (key_pos[None, :] <= query_pos[:, None]) & (
            query_users[:, None] == key_users[None, :]
        )

    def split_heads(values):
        return values.reshape(values.shape[0], HEADS, head_dim)

    def merge_heads(values):
        return values.reshape(values.shape[0], model_width)

    def piece_scores(query_part, key_part):
        return (
            jnp.einsum(
                "qhd,khd->hqk",
                split_heads(query_part),
                split_heads(key_part),
                preferred_element_type=jnp.float32,
            )
            * score_scale
        )

    rows_f = own_rows.astype(jnp.float32)
    normed, inverse_in = normalize(rows_f)
    normed_bf = normed.astype(jnp.bfloat16)
    pre = jnp.dot(normed_bf, proj_weight, preferred_element_type=jnp.float32)
    proj = (pre * jax.nn.sigmoid(pre)).astype(jnp.bfloat16)
    update_rows = proj[:, :model_width]
    value_rows = proj[:, model_width : 2 * model_width]
    query_rows = proj[:, 2 * model_width : 3 * model_width]
    key_rows = proj[:, 3 * model_width :]

    def attend_block(running, pieces, first_row):
        key_part, value_part = pieces
        key_pos = position_of(first_row + jnp.arange(key_part.shape[0], dtype=jnp.int32))
        allowed = allowed_of(own_pos, own_users, key_pos, user_of(key_pos))[None]
        scores = piece_scores(query_rows, key_part)
        weights = jnp.where(allowed, scores * jax.nn.sigmoid(scores), 0.0).astype(jnp.bfloat16)
        product = jnp.einsum(
            "hqk,khd->qhd", weights, split_heads(value_part), preferred_element_type=jnp.float32
        )
        return running + merge_heads(product)

    zeros_rows = jnp.zeros((row_count, model_width), jnp.float32)
    attended = in_blocks(
        attend_block,
        row_count,
        zeros_rows,
        (
            lax.all_gather(key_rows, "ctx", axis=0, tiled=True),
            lax.all_gather(value_rows, "ctx", axis=0, tiled=True),
        ),
    )
    att_normed, inverse_att = normalize(attended)
    update_f = update_rows.astype(jnp.float32)
    gated = (att_normed * update_f).astype(jnp.bfloat16)
    layer_rows = (rows_f + jnp.dot(gated, out_weight, preferred_element_type=jnp.float32)).astype(
        jnp.bfloat16
    )
    out_term = jnp.dot(gated.T, cotangent, preferred_element_type=jnp.float32)
    grad_gated = jnp.dot(cotangent, out_weight.T, preferred_element_type=jnp.float32)
    grad_update = grad_gated * att_normed
    grad_att = normalize_back(grad_gated * update_f, att_normed, inverse_att).astype(jnp.bfloat16)

    def query_block(running, pieces, first_row):
        key_part, value_part = pieces
        key_pos = position_of(first_row + jnp.arange(key_part.shape[0], dtype=jnp.int32))
        allowed = allowed_of(own_pos, own_users, key_pos, user_of(key_pos))[None]
        scores = piece_scores(query_rows, key_part)
        grad_weights = jnp.einsum(
            "qhd,khd->hqk",
            split_heads(grad_att),
            split_heads(value_part),
            preferred_element_type=jnp.float32,
        )
        grad_scores = jnp.where(
            allowed, grad_weights * silu_grad(scores) * score_scale, 0.0
        ).astype(jnp.bfloat16)
        product = jnp.einsum(
            "hqk,khd->qhd", grad_scores, split_heads(key_part), preferred_element_type=jnp.float32
        )
        return running + merge_heads(product)

    def key_block(running, pieces, first_row):
        query_part, grad_part = pieces
        query_pos = position_of(first_row + jnp.arange(query_part.shape[0], dtype=jnp.int32))
        allowed = allowed_of(query_pos, user_of(query_pos), own_pos, own_users)[None]
        scores = piece_scores(query_part, key_rows)
        weights = jnp.where(allowed, scores * jax.nn.sigmoid(scores), 0.0).astype(jnp.bfloat16)
        grad_weights = jnp.einsum(
            "qhd,khd->hqk",
            split_heads(grad_part),
            split_heads(value_rows),
            preferred_element_type=jnp.float32,
        )
        grad_scores = jnp.where(
            allowed, grad_weights * silu_grad(scores) * score_scale, 0.0
        ).astype(jnp.bfloat16)
        grad_key = jnp.einsum(
            "hqk,qhd->khd", grad_scores, split_heads(query_part), preferred_element_type=jnp.float32
        )
        grad_value = jnp.einsum(
            "hqk,qhd->khd", weights, split_heads(grad_part), preferred_element_type=jnp.float32
        )
        return (running[0] + merge_heads(grad_key), running[1] + merge_heads(grad_value))

    grad_query = in_blocks(
        query_block,
        row_count,
        zeros_rows,
        (
            lax.all_gather(key_rows, "ctx", axis=0, tiled=True),
            lax.all_gather(value_rows, "ctx", axis=0, tiled=True),
        ),
    )
    grad_key, grad_value = in_blocks(
        key_block,
        row_count,
        (zeros_rows, zeros_rows),
        (
            lax.all_gather(query_rows, "ctx", axis=0, tiled=True),
            lax.all_gather(grad_att, "ctx", axis=0, tiled=True),
        ),
    )
    grad_proj = jnp.concatenate([grad_update, grad_value, grad_query, grad_key], axis=1)
    grad_pre = (grad_proj * silu_grad(pre)).astype(jnp.bfloat16)
    proj_term = jnp.dot(normed_bf.T, grad_pre, preferred_element_type=jnp.float32)
    grad_normed = jnp.dot(grad_pre, proj_weight.T, preferred_element_type=jnp.float32)
    row_grads = (
        cotangent.astype(jnp.float32) + normalize_back(grad_normed, normed, inverse_in)
    ).astype(jnp.bfloat16)
    proj_sum, out_sum = lax.psum((proj_term, out_term), ("dp", "ctx"))
    grad_scale = (row_count * device_count) ** (-0.5)
    return (layer_rows, row_grads, proj_sum * grad_scale, out_sum * grad_scale)


def solution(mesh):
    placed = (
        P(("dp", "ctx"), None),
        P(("dp", "ctx")),
        P(("dp", "ctx")),
        P("dp", None),
        P(),
        P(),
        P(("dp", "ctx"), None),
    )
    return jax.shard_map(
        local,
        mesh=mesh,
        in_specs=placed,
        out_specs=(P(("dp", "ctx"), None), P(("dp", "ctx"), None), P(), P()),
        check_vma=False,
    )
```

profile of v0, /device:TPU:0, one launch (start us, length us, event | category | flops | bytes accessed | tf_op | source)
XLA Modules:
  0.0 400.7 jit_solution(9366824799308477023)
XLA Ops:
  8.0 2.0 scatter_custom_fusion
  10.9 7.3 %all-to-all-start = ((bf16[32,12,512]{2,1,0:T(8,128)(2,1)}), bf16[32,12,512]{2,1,0:T(8,128)(2,1)S(1)}, u32[]{:S(2)}, u32[]{:S(2)}) async-start(bf16[32,12,512]{2,1,0:T(8,128)(2,1)} %reshape.616), calls=%async_computation | async-start | bytes 1048576 | tf_op jit(solution)/shard_map/all_to_all | solution.py:55
  18.4 16.2 %all-to-all-done = bf16[32,12,512]{2,1,0:T(8,128)(2,1)S(1)} async-done(((bf16[32,12,512]{2,1,0:T(8,128)(2,1)}), bf16[32,12,512]{2,1,0:T(8,128)(2,1)S(1)}, u32[]{:S(2)}, u32[]{:S(2)}) %all-to-all-start) | async-done | bytes 393248 | tf_op jit(solution)/shard_map/all_to_all | solution.py:55
  34.6 1.2 gather_fusion
  36.2 2.1 multiply_convert_fusion
  41.3 1.8 copy.54
  43.1 1.8 copy.55
  45.8 18.7 %all-gather.5.cloned.1.call-done = bf16[1024,512]{1,0:T(8,128)(2,1)} async-done(((bf16[256,512]{1,0:T(8,128)(2,1)}), bf16[1024,512]{1,0:T(8,128)(2,1)}) %all-gather.5.cloned.1.call-update) | async-done | bytes 1048592 | tf_op jit(solution)/shard_map/all_gather | solution.py:133
  64.5 2.3 copy.48
  66.8 26.7 %all-gather.7.cloned.1.call-done = bf16[1024,512]{1,0:T(8,128)(2,1)} async-done(((bf16[256,512]{1,0:T(8,128)(2,1)}), bf16[1024,512]{1,0:T(8,128)(2,1)}) %all-gather.7.cloned.1.call-update) | async-done | bytes 1048592 | tf_op jit(solution)/shard_map/all_gather | solution.py:132
  93.5 2.3 copy.49
  95.7 17.4 %while.50 = (s32[]{:T(128)}, f32[256,512]{0,1:T(8,128)S(1)}, bf16[1024,512]{0,1:T(8,128)(2,1)}, s32[256]{0:T(256)S(1)}, s32[4]{0:T(128)S(1)}, /*index=5*/bf16[10...) while((s32[]{:T(128)}, f32[256,512]{0,1:T(8,128)S(1)}, ...), condition=%wide.region_7.8_spmd.clone, body=%wide.region_5.7_spmd.clone.sunk | while | flops 138364160 | bytes 4071625 | solution.py:35
  96.0 1.9 constant_dynamic-slice_fusion.10
  97.9 2.1 fusion.118
  100.4 1.9 constant_dynamic-slice_fusion.10
  102.2 2.1 fusion.118
  104.7 1.9 constant_dynamic-slice_fusion.10
  106.6 2.1 fusion.118
  109.1 1.9 constant_dynamic-slice_fusion.10
  111.0 2.1 fusion.118
  113.7 1.7 fusion.62
  115.4 2.1 multiply_convert_fusion.1
  118.6 46.4 %while.52 = (s32[]{:T(128)}, f32[256,512]{0,1:T(8,128)}, bf16[1024,512]{0,1:T(8,128)(2,1)}, s32[256]{0:T(256)S(1)}, s32[4]{0:T(128)S(1)}, /*index=5*/bf16[1024,5...) while((s32[]{:T(128)}, f32[256,512]{0,1:T(8,128)}, ...), condition=%wide.region_17.18_spmd.clone, body=%wide.region_15.17_spmd.clone.sunk | while | flops 208094464 | bytes 12984529 | solution.py:35
  119.9 3.2 fusion.133
  123.2 2.9 copy.73
  126.0 2.3 fusion.134
  130.7 3.2 fusion.133
  133.9 2.9 copy.73
  136.8 2.3 fusion.134
  139.2 2.0 bitcast_add_fusion.9
  141.4 1.2 constant_dynamic-slice_fusion.13
  142.7 3.2 fusion.133
  145.9 2.9 copy.73
  148.8 2.3 fusion.134
  151.1 2.0 bitcast_add_fusion.9
  154.5 3.2 fusion.133
  157.7 2.9 copy.73
  160.6 2.3 fusion.134
  163.0 2.0 bitcast_add_fusion.9
  164.9 2.1 copy.61
  167.0 2.3 fusion.70
  169.4 61.8 %while.51 = (s32[]{:T(128)}, f32[256,512]{0,1:T(8,128)S(1)}, f32[256,512]{0,1:T(8,128)}, bf16[1024,512]{1,0:T(8,128)(2,1)}, s32[4]{0:T(128)S(1)}, /*index=5*/s32...) while((s32[]{:T(128)}, f32[256,512]{0,1:T(8,128)S(1)}, ...), condition=%wide.region_14.15_spmd.clone, body=%wide.region_12.14_spmd.clone.sunk | while | flops 279135488 | bytes 18555156 | solution.py:35
  170.5 2.8 fusion.125
  175.4 3.8 fusion.127
  179.2 3.3 fusion.126
  182.5 1.6 bitcast_add_fusion.8
  185.9 2.8 fusion.125
  190.8 3.8 fusion.127
  194.6 3.3 fusion.126
  197.9 1.6 bitcast_add_fusion.8
  201.4 2.8 fusion.125
  206.2 3.8 fusion.127
  210.0 3.3 fusion.126
  213.3 1.6 bitcast_add_fusion.8
  216.8 2.8 fusion.125
  221.7 3.8 fusion.127
  225.5 3.3 fusion.126
  228.8 1.6 bitcast_add_fusion.8
  231.1 2.1 copy.60
  234.2 3.0 fusion.45
  237.2 2.9 fusion.63
  240.1 2.1 fusion.46
  244.1 144.0 %all-reduce.3.cloned.1.call-done = (f32[512,2048]{1,0:T(8,128)}, f32[512,512]{1,0:T(8,128)}) async-done(((f32[512,2048]{1,0:T(8,128)}, f32[512,512]{1,0:T(8,128)}), (f32[512,2048]{1,0:T(8,128)}, f32[512,512]{1,0:T(8,128)})) %all-reduce.3.cloned.1.call-update) | async-done | bytes 5242896 | tf_op jit(solution)/shard_map/psum | solution.py:214
  388.1 5.0 %broadcast_multiply_fusion = f32[512,2048]{1,0:T(8,128)} fusion(f32[512,2048]{1,0:T(8,128)} %get-tuple-element.919), kind=kLoop, calls=%fused_computation.106 | loop fusion | flops 1048576 | bytes 8388608 | tf_op jit(solution)/shard_map/mul | solution.py:216
  (141 shorter events, 34.2 us)
Async XLA Ops:
  7.2 29.0 %copy-start = (bf16[512,2048]{1,0:T(8,128)(2,1)S(1)}, bf16[512,2048]{1,0:T(8,128)(2,1)}, u32[]{:S(2)}) copy-start(bf16[512,2048]{1,0:T(8,128)(2,1)} %param.17) | copy-start | bytes 6291460
  7.2 11.1 %copy-start.9 = (s32[256]{0:T(256)S(1)}, s32[256]{0:T(256)}, u32[]{:S(2)}) copy-start(s32[256]{0:T(256)} %param.15) | copy-start | bytes 3076
  10.9 23.6 %all-to-all-start = ((bf16[32,12,512]{2,1,0:T(8,128)(2,1)}), bf16[32,12,512]{2,1,0:T(8,128)(2,1)S(1)}, u32[]{:S(2)}, u32[]{:S(2)}) async-start(bf16[32,12,512]{2,1,0:T(8,128)(2,1)} %reshape.616), calls=%async_computation | async-start | bytes 1048576 | tf_op jit(solution)/shard_map/all_to_all | solution.py:55
  18.3 46.2 %all-gather.5.cloned.1.call-start = ((), (), s32[]{:S(2)}) async-start(), calls=%async_computation.1 | async-start | bytes 1310720 | tf_op jit(solution)/shard_map/all_gather | solution.py:133
  38.3 1.0 copy-start.7
  38.3 2.7 copy-start.10
  40.1 5.6 %copy-start.5 = (bf16[256,512]{1,0:T(8,128)(2,1)}, bf16[256,512]{1,0:T(8,128)(2,1)S(1)}, u32[]{:S(2)}) copy-start(bf16[256,512]{1,0:T(8,128)(2,1)S(1)} %get-tuple-element.934) | copy-start | bytes 786436
  40.2 53.3 %all-gather.7.cloned.1.call-start = ((), (), s32[]{:S(2)}) async-start(), calls=%async_computation.2 | async-start | bytes 1310720 | tf_op jit(solution)/shard_map/all_gather | solution.py:132
  40.9 128.5 %all-gather.9.cloned.1.call-start = ((), (), s32[]{:S(2)}) async-start(), calls=%async_computation.3 | async-start | bytes 1310720 | tf_op jit(solution)/shard_map/all_gather | solution.py:203
  45.8 123.6 %all-gather.11.cloned.1.call-start = ((), (), s32[]{:S(2)}) async-start(), calls=%async_computation.4 | async-start | bytes 1310720 | tf_op jit(solution)/shard_map/all_gather | solution.py:204
  117.5 0.8 copy-start.4
  118.3 269.8 %all-reduce.3.cloned.1.call-start = ((), (), s32[]{:S(2)}) async-start(), calls=%async_computation.5 | async-start | bytes 10485760 | tf_op jit(solution)/shard_map/psum | solution.py:214
  164.9 4.4 %copy-start.1 = (f32[256,512]{0,1:T(8,128)S(1)}, f32[256,512]{0,1:T(8,128)}, u32[]{:S(2)}) copy-start(f32[256,512]{0,1:T(8,128)} %custom-call.1) | copy-start | bytes 1572868
  179.2 3.3 copy-start.2
  184.0 0.8 copy-start.3
  194.6 3.3 copy-start.2
  199.4 0.8 copy-start.3
  210.0 3.3 copy-start.2
  214.9 0.8 copy-start.3
  225.5 3.3 copy-start.2
  230.3 0.8 copy-start.3
  242.2 0.9 copy-start.6
  388.1 5.0 %copy-start.8 = (f32[512,512]{1,0:T(8,128)S(1)}, f32[512,512]{1,0:T(8,128)}, u32[]{:S(2)}) copy-start(f32[512,512]{1,0:T(8,128)} %get-tuple-element.920) | copy-start | bytes 3145732
Sparse Core Ops, SparseCore 0:
  40.3 24.1 all-gather.4
  66.9 26.4 all-gather.6
  95.3 26.5 all-gather.8
  123.6 26.4 all-gather.10
  240.2 147.8 all-reduce.2
where the time goes:
time: 403 us; the launch traced here: 401 us
  waiting for transfers between devices  206 us (51%)
  matrix products  82.1 us (20%)
  local copies, waits for them, and re-layouts  59.7 us (15%)
  other arithmetic  30.5 us (8%)
  between operations  14 us (3%)
  starting transfers between devices  7.71 us (2%)
    psum x1, waiting for transfers between devices, local(): proj_sum, out_sum = lax.psum((proj_term, out_term), ('dp', 'ctx'))  144 us
    all_gather x1, waiting for transfers between devices, local(): lax.all_gather(key_rows, 'ctx', axis=0, tiled=True)  26.7 us
    dot_general x8, matrix products, piece_scores(): jnp.einsum('qhd,khd->hqk', split_heads(query_part), split_heads(key_part)...  24.1 us
    dynamic_slice x24, local copies, waits for them, and re-layouts, one_block(): lax.dynamic_slice_in_dim(each, start, block_rows, 0)  23.5 us
    all_gather x1, waiting for transfers between devices, local(): lax.all_gather(value_rows, 'ctx', axis=0, tiled=True)  18.7 us
    all_to_all x1, waiting for transfers between devices, local(): lax.all_to_all(outgoing.reshape(device_count, capacity, model_width), ('d...  16.2 us
    dot_general x4, matrix products, key_block(): jnp.einsum('hqk,qhd->khd', grad_scores, split_heads(query_part), preferre...  15.2 us
    dot_general x4, matrix products, key_block(): jnp.einsum('hqk,qhd->khd', weights, split_heads(grad_part), preferred_ele...  13.1 us
  transfers between devices with their start and end apart: 6, of which 4 were waited for; matrix products, arithmetic and copies ran while one was open for 22% of the time, Pallas kernels for 0%

commit v1 on v0

--- a/solution.py
+++ b/solution.py
@@ -211,7 +211,7 @@
     row_grads = (
         cotangent.astype(jnp.float32) + normalize_back(grad_normed, normed, inverse_in)
     ).astype(jnp.bfloat16)
-    proj_sum, out_sum = lax.psum((proj_term, out_term), ("dp", "ctx"))
+    proj_sum, out_sum = lax.psum(lax.psum((proj_term, out_term), "ctx"), "dp")
     grad_scale = (row_count * device_count) ** (-0.5)
     return (layer_rows, row_grads, proj_sum * grad_scale, out_sum * grad_scale)
 

time: 403 us -> 494 us (1.23)
  waiting for transfers between devices: 206 us -> 298 us
    psum x1 -> x2, waiting for transfers between devices: 144 us -> 236 us  [local(): proj_sum, out_sum = lax.psum(lax.psum((proj_term, out_term), 'ctx'), 'dp')]
  transfers between devices with their start and end apart: 6 -> 7, of which waited for: 4 -> 5; matrix products, arithmetic and copies ran while one was open for 22% -> 17% of each run, Pallas kernels for 0% -> 0%
where the time goes in v1:
time: 494 us; the launch traced here: 492 us
  waiting for transfers between devices  298 us (60%)
  matrix products  81.9 us (17%)
  local copies, waits for them, and re-layouts  59.6 us (12%)
  other arithmetic  30.4 us (6%)
  between operations  14.3 us (3%)
  starting transfers between devices  7.75 us (2%)
    psum x2, waiting for transfers between devices, local(): proj_sum, out_sum = lax.psum(lax.psum((proj_term, out_term), 'ctx'), 'dp')  236 us
    all_gather x1, waiting for transfers between devices, local(): lax.all_gather(key_rows, 'ctx', axis=0, tiled=True)  26.7 us
    dot_general x8, matrix products, piece_scores(): jnp.einsum('qhd,khd->hqk', split_heads(query_part), split_heads(key_part)...  24 us
    dynamic_slice x24, local copies, waits for them, and re-layouts, one_block(): lax.dynamic_slice_in_dim(each, start, block_rows, 0)  23.5 us
    all_gather x1, waiting for transfers between devices, local(): lax.all_gather(value_rows, 'ctx', axis=0, tiled=True)  18.7 us
    all_to_all x1, waiting for transfers between devices, local(): lax.all_to_all(outgoing.reshape(device_count, capacity, model_width), ('d...  16.2 us
    dot_general x4, matrix products, key_block(): jnp.einsum('hqk,qhd->khd', grad_scores, split_heads(query_part), preferre...  15.2 us
    dot_general x4, matrix products, key_block(): jnp.einsum('hqk,qhd->khd', weights, split_heads(grad_part), preferred_ele...  13.1 us
  transfers between devices with their start and end apart: 7, of which 5 were waited for; matrix products, arithmetic and copies ran while one was open for 17% of the time, Pallas kernels for 0%

profile of v1, /device:TPU:0, one launch (start us, length us, event | category | flops | bytes accessed | tf_op | source)
XLA Modules:
  0.0 492.4 jit_solution(10365841640873411393)
XLA Ops:
  8.0 2.0 scatter_custom_fusion
  10.9 7.3 %all-to-all-start = ((bf16[32,12,512]{2,1,0:T(8,128)(2,1)}), bf16[32,12,512]{2,1,0:T(8,128)(2,1)S(1)}, u32[]{:S(2)}, u32[]{:S(2)}) async-start(bf16[32,12,512]{2,1,0:T(8,128)(2,1)} %reshape.616), calls=%async_computation | async-start | bytes 1048576 | tf_op jit(solution)/shard_map/all_to_all | solution.py:55
  18.4 16.2 %all-to-all-done = bf16[32,12,512]{2,1,0:T(8,128)(2,1)S(1)} async-done(((bf16[32,12,512]{2,1,0:T(8,128)(2,1)}), bf16[32,12,512]{2,1,0:T(8,128)(2,1)S(1)}, u32[]{:S(2)}, u32[]{:S(2)}) %all-to-all-start) | async-done | bytes 393248 | tf_op jit(solution)/shard_map/all_to_all | solution.py:55
  36.2 2.1 multiply_convert_fusion
  41.3 1.8 copy.54
  43.1 1.8 copy.55
  45.8 18.7 %all-gather.5.cloned.1.call-done = bf16[1024,512]{1,0:T(8,128)(2,1)} async-done(((bf16[256,512]{1,0:T(8,128)(2,1)}), bf16[1024,512]{1,0:T(8,128)(2,1)}) %all-gather.5.cloned.1.call-update) | async-done | bytes 1048592 | tf_op jit(solution)/shard_map/all_gather | solution.py:133
  64.5 2.3 copy.48
  66.8 26.7 %all-gather.7.cloned.1.call-done = bf16[1024,512]{1,0:T(8,128)(2,1)} async-done(((bf16[256,512]{1,0:T(8,128)(2,1)}), bf16[1024,512]{1,0:T(8,128)(2,1)}) %all-gather.7.cloned.1.call-update) | async-done | bytes 1048592 | tf_op jit(solution)/shard_map/all_gather | solution.py:132
  93.4 2.3 copy.49
  95.7 17.4 %while.50 = (s32[]{:T(128)}, f32[256,512]{0,1:T(8,128)S(1)}, bf16[1024,512]{0,1:T(8,128)(2,1)}, s32[256]{0:T(256)S(1)}, s32[4]{0:T(128)S(1)}, /*index=5*/bf16[10...) while((s32[]{:T(128)}, f32[256,512]{0,1:T(8,128)S(1)}, ...), condition=%wide.region_7.8_spmd.clone, body=%wide.region_5.7_spmd.clone.sunk | while | flops 138364160 | bytes 4071625 | solution.py:35
  96.0 1.9 constant_dynamic-slice_fusion.10
  97.8 2.1 fusion.118
  100.3 1.9 constant_dynamic-slice_fusion.10
  102.2 2.1 fusion.118
  104.7 1.9 constant_dynamic-slice_fusion.10
  106.6 2.1 fusion.118
  109.1 1.9 constant_dynamic-slice_fusion.10
  110.9 2.1 fusion.118
  113.7 1.7 fusion.62
  115.3 2.1 multiply_convert_fusion.1
  118.5 46.2 %while.52 = (s32[]{:T(128)}, f32[256,512]{0,1:T(8,128)}, bf16[1024,512]{0,1:T(8,128)(2,1)}, s32[256]{0:T(256)S(1)}, s32[4]{0:T(128)S(1)}, /*index=5*/bf16[1024,5...) while((s32[]{:T(128)}, f32[256,512]{0,1:T(8,128)}, ...), condition=%wide.region_17.18_spmd.clone, body=%wide.region_15.17_spmd.clone.sunk | while | flops 208094464 | bytes 12984529 | solution.py:35
  119.9 3.2 fusion.133
  123.1 2.9 copy.73
  126.0 2.3 fusion.134
  130.6 3.2 fusion.133
  133.9 2.9 copy.73
  136.7 2.3 fusion.134
  139.1 2.0 bitcast_add_fusion.9
  141.3 1.2 constant_dynamic-slice_fusion.13
  142.5 3.2 fusion.133
  145.8 2.9 copy.73
  148.6 2.3 fusion.134
  151.0 2.0 bitcast_add_fusion.9
  154.3 3.2 fusion.133
  157.5 2.9 copy.73
  160.4 2.3 fusion.134
  162.8 2.0 bitcast_add_fusion.9
  164.7 2.1 copy.61
  166.8 2.3 fusion.70
  169.2 61.7 %while.51 = (s32[]{:T(128)}, f32[256,512]{0,1:T(8,128)S(1)}, f32[256,512]{0,1:T(8,128)}, bf16[1024,512]{1,0:T(8,128)(2,1)}, s32[4]{0:T(128)S(1)}, /*index=5*/s32...) while((s32[]{:T(128)}, f32[256,512]{0,1:T(8,128)S(1)}, ...), condition=%wide.region_14.15_spmd.clone, body=%wide.region_12.14_spmd.clone.sunk | while | flops 279135488 | bytes 18555156 | solution.py:35
  170.3 2.8 fusion.125
  175.1 3.8 fusion.127
  178.9 3.3 fusion.126
  182.2 1.6 bitcast_add_fusion.8
  185.7 2.8 fusion.125
  190.6 3.8 fusion.127
  194.4 3.3 fusion.126
  197.6 1.6 bitcast_add_fusion.8
  201.1 2.8 fusion.125
  206.0 3.8 fusion.127
  209.8 3.3 fusion.126
  213.1 1.6 bitcast_add_fusion.8
  216.6 2.8 fusion.125
  221.4 3.8 fusion.127
  225.2 3.3 fusion.126
  228.5 1.6 bitcast_add_fusion.8
  230.9 2.0 copy.60
  233.9 3.0 fusion.45
  236.9 2.9 fusion.63
  239.8 121.0 %all-reduce.7.cloned.1.call-done = (f32[512,2048]{1,0:T(8,128)}, f32[512,512]{1,0:T(8,128)}) async-done(((f32[512,2048]{1,0:T(8,128)}, f32[512,512]{1,0:T(8,128)}), (f32[512,2048]{1,0:T(8,128)}, f32[512,512]{1,0:T(8,128)})) %all-reduce.7.cloned.1.call-update) | async-done | bytes 5242896 | tf_op jit(solution)/shard_map/psum | solution.py:214
  360.9 2.1 fusion.46
  364.9 114.5 %all-reduce.5.cloned.1.call-done = (f32[512,2048]{1,0:T(8,128)}, f32[512,512]{1,0:T(8,128)}) async-done(((f32[512,2048]{1,0:T(8,128)}, f32[512,512]{1,0:T(8,128)}), (f32[512,2048]{1,0:T(8,128)}, f32[512,512]{1,0:T(8,128)})) %all-reduce.5.cloned.1.call-update) | async-done | bytes 5242896 | tf_op jit(solution)/shard_map/psum | solution.py:214
  479.5 5.0 %broadcast_multiply_fusion = f32[512,2048]{1,0:T(8,128)} fusion(f32[512,2048]{1,0:T(8,128)} %get-tuple-element.919), kind=kLoop, calls=%fused_computation.106 | loop fusion | flops 1048576 | bytes 8388608 | tf_op jit(solution)/shard_map/mul | solution.py:216
  (144 shorter events, 35.4 us)
Async XLA Ops:
  7.2 29.0 %copy-start = (bf16[512,2048]{1,0:T(8,128)(2,1)S(1)}, bf16[512,2048]{1,0:T(8,128)(2,1)}, u32[]{:S(2)}) copy-start(bf16[512,2048]{1,0:T(8,128)(2,1)} %param.17) | copy-start | bytes 6291460
  7.2 11.1 %copy-start.9 = (s32[256]{0:T(256)S(1)}, s32[256]{0:T(256)}, u32[]{:S(2)}) copy-start(s32[256]{0:T(256)} %param.15) | copy-start | bytes 3076
  10.9 23.6 %all-to-all-start = ((bf16[32,12,512]{2,1,0:T(8,128)(2,1)}), bf16[32,12,512]{2,1,0:T(8,128)(2,1)S(1)}, u32[]{:S(2)}, u32[]{:S(2)}) async-start(bf16[32,12,512]{2,1,0:T(8,128)(2,1)} %reshape.616), calls=%async_computation | async-start | bytes 1048576 | tf_op jit(solution)/shard_map/all_to_all | solution.py:55
  18.3 46.2 %all-gather.5.cloned.1.call-start = ((), (), s32[]{:S(2)}) async-start(), calls=%async_computation.1 | async-start | bytes 1310720 | tf_op jit(solution)/shard_map/all_gather | solution.py:133
  38.3 1.0 copy-start.7
  38.3 2.7 copy-start.10
  40.1 5.6 %copy-start.5 = (bf16[256,512]{1,0:T(8,128)(2,1)}, bf16[256,512]{1,0:T(8,128)(2,1)S(1)}, u32[]{:S(2)}) copy-start(bf16[256,512]{1,0:T(8,128)(2,1)S(1)} %get-tuple-element.936) | copy-start | bytes 786436
  40.1 53.3 %all-gather.7.cloned.1.call-start = ((), (), s32[]{:S(2)}) async-start(), calls=%async_computation.2 | async-start | bytes 1310720 | tf_op jit(solution)/shard_map/all_gather | solution.py:132
  40.9 128.3 %all-gather.9.cloned.1.call-start = ((), (), s32[]{:S(2)}) async-start(), calls=%async_computation.3 | async-start | bytes 1310720 | tf_op jit(solution)/shard_map/all_gather | solution.py:203
  45.7 123.5 %all-gather.11.cloned.1.call-start = ((), (), s32[]{:S(2)}) async-start(), calls=%async_computation.4 | async-start | bytes 1310720 | tf_op jit(solution)/shard_map/all_gather | solution.py:204
  117.4 0.8 copy-start.4
  118.3 242.6 %all-reduce.7.cloned.1.call-start = ((), (), s32[]{:S(2)}) async-start(), calls=%async_computation.6 | async-start | bytes 10485760 | tf_op jit(solution)/shard_map/psum | solution.py:214
  164.7 4.4 copy-start.1
  178.9 3.3 copy-start.2
  183.8 0.8 copy-start.3
  194.4 3.3 copy-start.2
  199.2 0.8 copy-start.3
  209.8 3.3 copy-start.2
  214.6 0.8 copy-start.3
  225.2 3.3 copy-start.2
  230.0 0.8 copy-start.3
  239.8 239.7 %all-reduce.5.cloned.1.call-start = ((), (), s32[]{:S(2)}) async-start(), calls=%async_computation.5 | async-start | bytes 10485760 | tf_op jit(solution)/shard_map/psum | solution.py:214
  363.0 0.9 copy-start.6
  479.5 5.0 %copy-start.8 = (f32[512,512]{1,0:T(8,128)S(1)}, f32[512,512]{1,0:T(8,128)}, u32[]{:S(2)}) copy-start(f32[512,512]{1,0:T(8,128)} %get-tuple-element.920) | copy-start | bytes 3145732
Sparse Core Ops, SparseCore 0:
  40.3 24.1 all-gather.4
  66.9 26.4 all-gather.6
  95.3 26.5 all-gather.8
  123.5 26.4 all-gather.10
  239.9 120.9 all-reduce.6
  363.2 116.2 all-reduce.4
